TPU v7x, 128 devices: a whole 4x4x4 slice. The times are simulated.
128 devices in a mesh: row: 8 (over z, core), col: 16 (over x, y).
Axes of the slice: x: 4, y: 4, z: 4, core: 2. Of those that a mesh axis runs over, the one named last changes fastest.
Arguments:
- embed: bfloat16 [262144, 64], P(('row', 'col')), may hold values from -6 to 6
- tiles: bfloat16 [8192, 128, 128], P(('row', 'col'))
- tile_rows: int32 [8192], P(('row', 'col')), may hold values from 0 to 2047, as said below
- tile_cols: int32 [8192], P(('row', 'col')), may hold values from 0 to 2047, as said below
- chg_tiles: bfloat16 [24576, 128, 128], P(('row', 'col'))
- chg_rows: int32 [24576], P(('row', 'col')), may hold values from 0 to 2047, as said below
- chg_cols: int32 [24576], P(('row', 'col')), may hold values from 0 to 2047, as said below
Outputs:
- embedding: float32 [262144, 64], P(('row', 'col'))
Inputs may be any that keep to these rules, and one draw needn't show every extreme that they name: Tile n lies in the row group of the device that holds it: tile_rows[n] // 256 equals (n // 64) // 16. Tile n lies in the column group of the device that holds it: tile_cols[n] // 128 equals (n // 64) % 16. `chg_rows`: one device's list names each transpose owner at most 3 times; in every draw some owner is named exactly 3 times by every device's list. `chg_cols`: read with chg_rows to give the transpose owner.
All inputs are finite; a program needn't handle non-finite values.
Results may differ from a plain program's by a relative error of at most 0.025.
Values may be sent and summed in bfloat16 or wider, within the bound.
A program may use at most 192 MiB of HBM per device.

v0:
```python
import jax
import jax.numpy as jnp
from jax import lax
from jax.sharding import PartitionSpec as P

ITERS = 3
CAP = 3


def block_terms(own, own_rows, own_cols, taken, taken_rows, taken_cols, blocked, row_blocks):
    own_terms = jnp.einsum(
        "nab,nbk->nak", own, blocked[own_cols], preferred_element_type=jnp.float32
    )
    taken_terms = jnp.einsum(
        "nab,nak->nbk", taken, blocked[taken_cols], preferred_element_type=jnp.float32
    )
    return jax.ops.segment_sum(own_terms, own_rows, row_blocks) + jax.ops.segment_sum(
        taken_terms, taken_rows, row_blocks
    )


def local(embed, tiles, tile_rows, tile_cols, chg_tiles, chg_rows, chg_cols):
    rows_dev, feature_width = embed.shape
    tile_size = tiles.shape[1]
    row_count = lax.axis_size("row")
    col_count = lax.axis_size("col")
    devices = row_count * col_count
    row_blocks = rows_dev * col_count // tile_size
    col_blocks = rows_dev * row_count // tile_size
    sub_rows = rows_dev // devices
    owners = chg_cols // row_blocks * col_count + chg_rows // col_blocks
    position = jnp.arange(owners.shape[0], dtype=jnp.int32)
    earlier = position[None, :] < position[:, None]
    slot_rank = jnp.sum(jnp.logical_and(owners[:, None] == owners[None, :], earlier), axis=1)
    outgoing = (
        jnp.zeros((devices, CAP, tile_size, tile_size), jnp.bfloat16)
        .at[owners, slot_rank]
        .set(chg_tiles)
    )
    placing = jnp.stack([chg_cols % row_blocks, chg_rows % col_blocks], axis=1)
    output_slots = jnp.zeros((devices, CAP, 2), jnp.int32).at[owners, slot_rank].set(placing)
    taken, taken_places = (
        lax.all_to_all(outgoing, ("row", "col"), split_axis=0, concat_axis=0, tiled=True),
        lax.all_to_all(output_slots, ("row", "col"), split_axis=0, concat_axis=0, tiled=True),
    )
    taken = taken.reshape(devices * CAP, tile_size, tile_size)
    taken_places = taken_places.reshape(devices * CAP, 2)
    taken_rows = taken_places[:, 0]
    taken_cols = taken_places[:, 1]
    own_rows = tile_rows % row_blocks
    own_cols = tile_cols % col_blocks
    degree_terms = jax.ops.segment_sum(
        jnp.sum(jnp.abs(tiles), axis=2, dtype=jnp.float32), own_rows, row_blocks
    )
    degree_terms = degree_terms + jax.ops.segment_sum(
        jnp.sum(jnp.abs(taken), axis=1, dtype=jnp.float32), taken_rows, row_blocks
    )
    degree = 1.0 + lax.psum_scatter(
        degree_terms.astype(jnp.bfloat16), "col", scatter_dimension=0, tiled=True
    ).astype(jnp.float32).reshape(rows_dev, 1)
    nodes = rows_dev * devices
    current = embed
    final_output = embed.astype(jnp.float32)
    for iteration in range(ITERS):
        received_terms = lax.all_to_all(
            current.reshape(devices, sub_rows, feature_width),
            ("row", "col"),
            split_axis=0,
            concat_axis=0,
            tiled=True,
        )
        group = lax.all_gather(
            received_terms.reshape(rows_dev, feature_width), "row", axis=0, tiled=True
        )
        blocked = group.reshape(col_blocks, tile_size, feature_width)
        partial_value = block_terms(
            tiles, own_rows, own_cols, taken, taken_rows, taken_cols, blocked, row_blocks
        )
        summed = lax.psum_scatter(
            partial_value.reshape(row_blocks * tile_size, feature_width).astype(jnp.bfloat16),
            "col",
            scatter_dimension=0,
            tiled=True,
        ).astype(jnp.float32)
        scaled = summed / degree
        local_gram = jnp.dot(
            scaled.T, scaled, precision=lax.Precision.HIGHEST, preferred_element_type=jnp.float32
        )
        gram = lax.psum(local_gram, ("row", "col")) / nodes
        lower = jnp.linalg.cholesky(gram)
        final_output = lax.linalg.triangular_solve(
            lower, scaled, left_side=False, lower=True, transpose_a=True
        )
        current = final_output.astype(jnp.bfloat16)
    return final_output


def solution(mesh):
    placed = (
        P(("row", "col"), None),
        P(("row", "col"), None, None),
        P(("row", "col")),
        P(("row", "col")),
        P(("row", "col"), None, None),
        P(("row", "col")),
        P(("row", "col")),
    )
    return jax.shard_map(
        local, mesh=mesh, in_specs=placed, out_specs=P(("row", "col"), None), check_vma=False
    )
```

profile of v0, /device:TPU:1, one launch (start us, length us, event | category | flops | bytes accessed | tf_op | source)
XLA Modules:
  0.0 1204.5 jit_solution(14980614209809009102)
XLA Ops:
  8.4 10.1 scatter_fusion.1
  18.5 1.5 copy.79
  20.0 11.5 all-to-all-start.1
  31.6 1.2 copy.75
  33.8 7.8 all-to-all-done.1
  41.6 4.1 all-to-all-start
  45.7 7.7 broadcast_in_dim.14
  53.4 30.8 %scatter_fusion.2 = bf16[128,3,128,128]{3,2,1,0:T(8,128)(2,1)} fusion(bf16[128,3,128,128]{3,2,1,0:T(8,128)(2,1)} %broadcast_in_dim.14, s32[192]{0:T(256)S(1)} %bitcast.91, bf16[192,128,128]{2,1,0:T(8,128)(2,1)} %param.14), kind=kCustom, calls=%fused_computation.8 | custom fusion | bytes 18875904 | tf_op jit(solution)/shard_map/scatter | solution.py:38
  84.2 10.2 all-to-all-start.2
  94.5 1.1 reshape.236
  97.6 142.3 %all-gather.4.cloned.1.call-done = bf16[16384,64]{1,0:T(8,128)(2,1)} async-done(((bf16[2048,64]{1,0:T(8,128)(2,1)}), bf16[16384,64]{1,0:T(8,128)(2,1)}) %all-gather.4.cloned.1.call-update) | async-done | bytes 2097168 | tf_op jit(solution)/shard_map/all_gather | solution.py:72
  239.9 3.9 copy.77
  243.8 13.3 %gather_fusion.1 = bf16[384,128,64]{1,2,0:T(8,128)(2,1)} fusion(bf16[128,128,64]{1,2,0:T(8,128)(2,1)S(1)} %copy.77, s32[1024]{0:T(1024)S(1)} %pad_clamp_fusion), kind=kCustom, calls=%fused_computation.1 | custom fusion | bytes 12584448 | tf_op jit(solution)/shard_map/gather | solution.py:15
  257.8 3.1 convolution_bitcast_fusion.5
  260.9 4.3 broadcast.110.clone.2
  265.2 9.0 scatter_fusion
  274.2 9.2 convert_reduce_fusion
  283.5 2.5 scatter_custom_fusion.5
  286.7 14.3 %fusion.38 = f32[384,128,64]{1,2,0:T(8,128)} fusion(bf16[384,128,64]{1,2,0:T(8,128)(2,1)} %gather_fusion.1, bf16[384,128,128]{2,1,0:T(8,128)(2,1)} %bitcast.9), kind=kOutput, calls=%fused_computation.120 | convolution fusion | flops 805306368 | bytes 31457280 | tf_op jit(solution)/shard_map/nab,nak->nbk/dot_general | solution.py:14
  301.0 4.3 broadcast.110.clone.3
  305.3 59.8 %scatter_fusion.3 = f32[256,128,64]{1,2,0:T(8,128)} fusion(f32[256,128,64]{1,2,0:T(8,128)} %broadcast.110.clone.3, s32[384]{0:T(512)S(1)} %get-tuple-element.8, f32[384,128,64]{1,2,0:T(8,128)} %fusion.38), kind=kCustom, calls=%fused_computation.9 | custom fusion | flops 3145728 | bytes 37750272 | tf_op jit(solution)/shard_map/scatter-add | solution.py:17
  365.1 8.6 copy_bitcast_fusion.2
  375.0 8.3 all-reduce.3.cloned.1.call-done
  384.0 84.0 %reduce-scatter.4.cloned.1.call-done = bf16[2048,64]{0,1:T(8,128)(2,1)} async-done(((bf16[32768,64]{0,1:T(8,128)(2,1)}), bf16[2048,64]{0,1:T(8,128)(2,1)}) %reduce-scatter.4.cloned.1.call-update) | async-done | bytes 262160 | tf_op jit(solution)/shard_map/reduce_scatter | solution.py:79
  468.0 1.7 fusion.5
  469.7 66.1 %psum.21 = f32[64,64]{0,1:T(8,128)S(1)} all-reduce(f32[64,64]{0,1:T(8,128)S(1)} %fusion.5), channel_id=1, replica_groups=mesh['row'=8,'col'=16] {'row','col'}, use_global_device_ids=true, to_apply=%region_11.12 | all-reduce | flops 4096 | bytes 32768 | tf_op jit(solution)/shard_map/psum | solution.py:89
  535.9 5.8 cholesky.59
  543.1 4.9 custom-call.11
  548.0 1.6 fusion.3
  550.2 15.7 %all_to_all.25 = bf16[128,2,512]{2,1,0:T(2,128)(2,1)S(1)} all-to-all(bf16[128,2,512]{2,1,0:T(2,128)(2,1)S(1)} %reshape.237), channel_id=1, replica_groups=mesh['row'=8,'col'=16] {'row','col'}, dimensions={0} | all-to-all | bytes 524288 | tf_op jit(solution)/shard_map/all_to_all | solution.py:65
  565.9 1.1 reshape.238
  567.3 28.7 %all-gather.6.cloned.1.call-done = bf16[16384,64]{1,0:T(8,128)(2,1)} async-done(((bf16[2048,64]{1,0:T(8,128)(2,1)}), bf16[16384,64]{1,0:T(8,128)(2,1)}) %all-gather.6.cloned.1.call-update) | async-done | bytes 2097168 | tf_op jit(solution)/shard_map/all_gather | solution.py:72
  595.9 3.7 copy.87
  599.6 13.3 %gather_fusion.3 = bf16[384,128,64]{1,2,0:T(8,128)(2,1)} fusion(bf16[128,128,64]{1,2,0:T(8,128)(2,1)S(1)} %copy.87, s32[1024]{0:T(1024)S(1)} %pad_clamp_fusion), kind=kCustom, calls=%fused_computation.3 | custom fusion | bytes 12584448 | tf_op jit(solution)/shard_map/gather | solution.py:15
  613.7 14.4 %fusion.39 = f32[384,128,64]{1,2,0:T(8,128)} fusion(bf16[384,128,64]{1,2,0:T(8,128)(2,1)} %gather_fusion.3, bf16[384,128,128]{2,1,0:T(8,128)(2,1)} %bitcast.9), kind=kOutput, calls=%fused_computation.121 | convolution fusion | flops 805306368 | bytes 31457280 | tf_op jit(solution)/shard_map/nab,nak->nbk/dot_general | solution.py:14
  628.1 1.5 convolution_bitcast_fusion.4
  629.6 4.3 broadcast.110.clone.4
  633.9 59.8 %scatter_fusion.5 = f32[256,128,64]{1,2,0:T(8,128)} fusion(f32[256,128,64]{1,2,0:T(8,128)} %broadcast.110.clone.4, s32[384]{0:T(512)S(1)} %get-tuple-element.8, f32[384,128,64]{1,2,0:T(8,128)} %fusion.39), kind=kCustom, calls=%fused_computation.13 | custom fusion | flops 3145728 | bytes 37750272 | tf_op jit(solution)/shard_map/scatter-add | solution.py:17
  693.7 4.3 broadcast.110.clone.1
  698.0 9.2 scatter_fusion.4
  707.2 8.6 copy_bitcast_fusion.1
  715.9 75.9 %reduce-scatter.6.cloned.1.call-done = bf16[2048,64]{0,1:T(8,128)(2,1)} async-done(((bf16[32768,64]{0,1:T(8,128)(2,1)}), bf16[2048,64]{0,1:T(8,128)(2,1)}) %reduce-scatter.6.cloned.1.call-update) | async-done | bytes 262160 | tf_op jit(solution)/shard_map/reduce_scatter | solution.py:79
  791.8 1.7 fusion.6
  793.4 66.2 %psum.22 = f32[64,64]{0,1:T(8,128)S(1)} all-reduce(f32[64,64]{0,1:T(8,128)S(1)} %fusion.6), channel_id=1, replica_groups=mesh['row'=8,'col'=16] {'row','col'}, use_global_device_ids=true, to_apply=%region_17.20 | all-reduce | flops 4096 | bytes 32768 | tf_op jit(solution)/shard_map/psum | solution.py:89
  859.7 5.8 cholesky.70
  866.9 4.9 custom-call.12
  871.8 1.6 fusion.4
  873.9 15.7 %all_to_all.26 = bf16[128,2,512]{2,1,0:T(2,128)(2,1)S(1)} all-to-all(bf16[128,2,512]{2,1,0:T(2,128)(2,1)S(1)} %reshape.239), channel_id=1, replica_groups=mesh['row'=8,'col'=16] {'row','col'}, dimensions={0} | all-to-all | bytes 524288 | tf_op jit(solution)/shard_map/all_to_all | solution.py:65
  890.9 28.8 %all-gather.8.cloned.1.call-done = bf16[16384,64]{1,0:T(8,128)(2,1)} async-done(((bf16[2048,64]{1,0:T(8,128)(2,1)}), bf16[16384,64]{1,0:T(8,128)(2,1)}) %all-gather.8.cloned.1.call-update) | async-done | bytes 2097168 | tf_op jit(solution)/shard_map/all_gather | solution.py:72
  919.7 3.7 copy.94
  923.4 13.3 %gather_fusion.5 = bf16[384,128,64]{1,2,0:T(8,128)(2,1)} fusion(bf16[128,128,64]{1,2,0:T(8,128)(2,1)S(1)} %copy.94, s32[1024]{0:T(1024)S(1)} %pad_clamp_fusion), kind=kCustom, calls=%fused_computation.5 | custom fusion | bytes 12584448 | tf_op jit(solution)/shard_map/gather | solution.py:15
  937.5 14.4 %fusion.40 = f32[384,128,64]{1,2,0:T(8,128)} fusion(bf16[384,128,64]{1,2,0:T(8,128)(2,1)} %gather_fusion.5, bf16[384,128,128]{2,1,0:T(8,128)(2,1)} %bitcast.9), kind=kOutput, calls=%fused_computation.122 | convolution fusion | flops 805306368 | bytes 31457280 | tf_op jit(solution)/shard_map/nab,nak->nbk/dot_general | solution.py:14
  951.9 1.5 convolution_bitcast_fusion.3
  953.4 4.3 broadcast.110.clone.5
  957.7 58.9 %scatter_fusion.7 = f32[256,128,64]{1,2,0:T(8,128)} fusion(f32[256,128,64]{1,2,0:T(8,128)} %broadcast.110.clone.5, s32[384]{0:T(512)S(1)} %get-tuple-element.8, f32[384,128,64]{1,2,0:T(8,128)} %fusion.40), kind=kCustom, calls=%fused_computation.15 | custom fusion | flops 3145728 | bytes 37750272 | tf_op jit(solution)/shard_map/scatter-add | solution.py:17
  1016.6 4.3 broadcast.110.clone
  1020.9 9.2 scatter_fusion.6
  1030.1 8.5 copy_bitcast_fusion
  1038.7 75.5 %reduce-scatter.8.cloned.1.call-done = bf16[2048,64]{0,1:T(8,128)(2,1)} async-done(((bf16[32768,64]{0,1:T(8,128)(2,1)}), bf16[2048,64]{0,1:T(8,128)(2,1)}) %reduce-scatter.8.cloned.1.call-update) | async-done | bytes 262160 | tf_op jit(solution)/shard_map/reduce_scatter | solution.py:79
  1114.2 1.7 fusion.7
  1115.9 66.3 %psum.23 = f32[64,64]{0,1:T(8,128)S(1)} all-reduce(f32[64,64]{0,1:T(8,128)S(1)} %fusion.7), channel_id=1, replica_groups=mesh['row'=8,'col'=16] {'row','col'}, use_global_device_ids=true, to_apply=%region_21.24 | all-reduce | flops 4096 | bytes 32768 | tf_op jit(solution)/shard_map/psum | solution.py:89
  1182.2 5.8 cholesky.81
  1189.4 4.9 custom-call.13
  1194.3 2.4 convolution_bitcast_fusion
  (74 shorter events, 15.2 us)
Async XLA Ops:
  20.0 21.6 %all-to-all-start.1 = ((s32[128,3,2]{1,2,0:T(2,128)}), s32[128,3,2]{1,2,0:T(2,128)S(1)}, u32[]{:S(2)}, u32[]{:S(2)}) async-start(s32[128,3,2]{1,2,0:T(2,128)} %copy.79), calls=%async_computation.1 | async-start | bytes 262144 | tf_op jit(solution)/shard_map/all_to_all | solution.py:44
  41.6 42.6 %all-to-all-start = ((bf16[128,2,512]{2,1,0:T(2,128)(2,1)}), bf16[128,2,512]{2,1,0:T(2,128)(2,1)S(1)}, u32[]{:S(2)}, u32[]{:S(2)}) async-start(bf16[128,2,512]{2,1,0:T(2,128)(2,1)} %reshape.235), calls=%async_computation | async-start | bytes 524288 | tf_op jit(solution)/shard_map/all_to_all | solution.py:65
  84.2 11.5 copy-start.3
  84.2 11.6 copy-start
  84.2 13.1 %copy-start.4 = (s32[64]{0:T(128)S(1)}, s32[64]{0:T(128)}, u32[]{:S(2)}) copy-start(s32[64]{0:T(128)} %param.13) | copy-start | bytes 772
  84.2 190.0 %all-to-all-start.2 = ((bf16[128,3,128,128]{3,2,1,0:T(8,128)(2,1)}), bf16[128,3,128,128]{3,2,1,0:T(8,128)(2,1)}, u32[]{:S(2)}, u32[]{:S(2)}) async-start(bf16[128,3,128,128]{3,2,1,0:T(8,128)(2,1)} %scatter_fusion.2), calls=%async_computation.2 | async-start | bytes 25165824 | tf_op jit(solution)/shard_map/all_to_all | solution.py:43
  94.5 145.4 %all-gather.4.cloned.1.call-start = ((), (), s32[]{:S(2)}) async-start(), calls=%async_computation.8 | async-start | bytes 4718592 | tf_op jit(solution)/shard_map/all_gather | solution.py:72
  95.7 287.6 %all-reduce.3.cloned.1.call-start = ((), (), s32[]{:S(2)}) async-start(), calls=%async_computation.14 | async-start | bytes 131072
  286.7 181.4 %reduce-scatter.4.cloned.1.call-start = ((), (), s32[]{:S(2)}) async-start(), calls=%async_computation.9 | async-start | bytes 4456448 | tf_op jit(solution)/shard_map/reduce_scatter | solution.py:79
  365.1 8.7 copy-start.5
  373.7 222.2 %all-gather.6.cloned.1.call-start = ((), (), s32[]{:S(2)}) async-start(), calls=%async_computation.10 | async-start | bytes 4718592 | tf_op jit(solution)/shard_map/all_gather | solution.py:72
  567.1 224.7 %reduce-scatter.6.cloned.1.call-start = ((), (), s32[]{:S(2)}) async-start(), calls=%async_computation.11 | async-start | bytes 4456448 | tf_op jit(solution)/shard_map/reduce_scatter | solution.py:79
  613.7 14.4 %copy-start.1 = (bf16[64,128,128]{2,1,0:T(8,128)(2,1)S(1)}, bf16[64,128,128]{2,1,0:T(8,128)(2,1)}, u32[]{:S(2)}) copy-start(bf16[64,128,128]{2,1,0:T(8,128)(2,1)} %param.11) | copy-start | bytes 6291460
  715.8 203.9 %all-gather.8.cloned.1.call-start = ((), (), s32[]{:S(2)}) async-start(), calls=%async_computation.12 | async-start | bytes 4718592 | tf_op jit(solution)/shard_map/all_gather | solution.py:72
  890.8 223.4 %reduce-scatter.8.cloned.1.call-start = ((), (), s32[]{:S(2)}) async-start(), calls=%async_computation.13 | async-start | bytes 4456448 | tf_op jit(solution)/shard_map/reduce_scatter | solution.py:79
  937.5 14.4 %copy-start.2 = (bf16[64,128,128]{2,1,0:T(8,128)(2,1)S(1)}, bf16[64,128,128]{2,1,0:T(8,128)(2,1)}, u32[]{:S(2)}) copy-start(bf16[64,128,128]{2,1,0:T(8,128)(2,1)} %param.11) | copy-start | bytes 6291460
Sparse Core Ops, SparseCore 0:
  97.1 142.6 all-gather.3
  567.2 28.7 all-gather.5
  891.0 28.7 all-gather.7
Sparse Core Ops, SparseCore 1:
  286.7 96.5 all-reduce.2
  386.9 81.1 reduce-scatter.3
  715.9 75.8 reduce-scatter.5
  1038.8 75.4 reduce-scatter.7
where the time goes:
time: 1210 us; the launch traced here: 1200 us
  waiting for transfers between devices  451 us (37%)
  other arithmetic  283 us (23%)
  blocking collectives  230 us (19%)
  local copies, waits for them, and re-layouts  137 us (11%)
  matrix products  59.8 us (5%)
  starting transfers between devices  26.3 us (2%)
  between operations  16.4 us (1%)
    reduce_scatter x3, waiting for transfers between devices, local(): lax.psum_scatter(partial_value.reshape(row_blocks * tile_size, feature_wi...  235 us
    all_gather x3, waiting for transfers between devices, local(): lax.all_gather(received_terms.reshape(rows_dev, feature_width), 'row', ax...  200 us
    psum x3, blocking collectives, local(): gram = lax.psum(local_gram, ('row', 'col')) / nodes  199 us
    scatter-add x3, other arithmetic, block_terms(): jax.ops.segment_sum(taken_terms, taken_rows, row_blocks)  179 us
    dot_general x3, matrix products, block_terms(): jnp.einsum('nab,nak->nbk', taken, blocked[taken_cols], preferred_element_...  43.1 us
    gather x3, local copies, waits for them, and re-layouts, block_terms(): blocked[taken_cols]  39.8 us
    all_to_all x2, blocking collectives, local(): lax.all_to_all(current.reshape(devices, sub_rows, feature_width), ('row',...  31.5 us
    scatter x1, local copies, waits for them, and re-layouts, local(): outgoing = jnp.zeros((devices, CAP, tile_size, tile_size), jnp.bfloat16)....  30.8 us
  transfers between devices with their start and end apart: 10, of which 8 were waited for; matrix products, arithmetic and copies ran while one was open for 14% of the time, Pallas kernels for 0%

commit v1 on v0

--- a/solution.py
+++ b/solution.py
@@ -86,7 +86,10 @@
         local_gram = jnp.dot(
             scaled.T, scaled, precision=lax.Precision.HIGHEST, preferred_element_type=jnp.float32
         )
-        gram = lax.psum(local_gram, ("row", "col")) / nodes
+        row_try_all = lambda my_data, shard_axis: jnp.sum(
+            lax.all_gather(my_data, shard_axis), axis=0
+        )
+        gram = row_try_all(local_gram, ("row", "col")) / nodes
         lower = jnp.linalg.cholesky(gram)
         final_output = lax.linalg.triangular_solve(
             lower, scaled, left_side=False, lower=True, transpose_a=True

time: 1210 us -> 1230 us (1.017)
  waiting for transfers between devices: 451 us -> 657 us
  blocking collectives: 230 us -> 32.6 us
    all_gather x0 -> x3, waiting for transfers between devices: none -> 205 us  [local(): lax.all_gather(my_data, shard_axis)]
    psum x3 -> x0, blocking collectives: 199 us -> none  [local(): gram = lax.psum(local_gram, ('row', 'col')) / nodes]
  transfers between devices with their start and end apart: 10 -> 13, of which waited for: 8 -> 11; matrix products, arithmetic and copies ran while one was open for 14% -> 14% of each run, Pallas kernels for 0% -> 0%
where the time goes in v1:
time: 1230 us; the launch traced here: 1220 us
  waiting for transfers between devices  657 us (53%)
  other arithmetic  291 us (24%)
  local copies, waits for them, and re-layouts  138 us (11%)
  matrix products  59 us (5%)
  blocking collectives  32.6 us (3%)
  starting transfers between devices  26.3 us (2%)
  between operations  16.7 us (1%)
    reduce_scatter x3, waiting for transfers between devices, local(): lax.psum_scatter(partial_value.reshape(row_blocks * tile_size, feature_wi...  235 us
    all_gather x3, waiting for transfers between devices, local(): lax.all_gather(my_data, shard_axis)  205 us
    all_gather x3, waiting for transfers between devices, local(): lax.all_gather(received_terms.reshape(rows_dev, feature_width), 'row', ax...  200 us
    scatter-add x3, other arithmetic, block_terms(): jax.ops.segment_sum(taken_terms, taken_rows, row_blocks)  179 us
    dot_general x3, matrix products, block_terms(): jnp.einsum('nab,nak->nbk', taken, blocked[taken_cols], preferred_element_...  43.1 us
    gather x3, local copies, waits for them, and re-layouts, block_terms(): blocked[taken_cols]  39.8 us
    all_to_all x2, blocking collectives, local(): lax.all_to_all(current.reshape(devices, sub_rows, feature_width), ('row',...  32.6 us
    scatter x1, local copies, waits for them, and re-layouts, local(): outgoing = jnp.zeros((devices, CAP, tile_size, tile_size), jnp.bfloat16)....  30.8 us
  transfers between devices with their start and end apart: 13, of which 11 were waited for; matrix products, arithmetic and copies ran while one was open for 14% of the time, Pallas kernels for 0%

profile of v1, /device:TPU:1, one launch (start us, length us, event | category | flops | bytes accessed | tf_op | source)
XLA Modules:
  0.0 1219.7 jit_solution(14361753959178189297)
XLA Ops:
  8.4 10.1 scatter_fusion.1
  18.5 1.5 copy.70
  20.0 11.5 all-to-all-start.1
  31.6 1.2 copy.66
  33.8 7.8 all-to-all-done.1
  41.6 4.1 all-to-all-start
  45.7 7.7 broadcast_in_dim.14
  53.4 30.8 %scatter_fusion.2 = bf16[128,3,128,128]{3,2,1,0:T(8,128)(2,1)} fusion(bf16[128,3,128,128]{3,2,1,0:T(8,128)(2,1)} %broadcast_in_dim.14, s32[192]{0:T(256)S(1)} %bitcast.94, bf16[192,128,128]{2,1,0:T(8,128)(2,1)} %param.14), kind=kCustom, calls=%fused_computation.8 | custom fusion | bytes 18875904 | tf_op jit(solution)/shard_map/scatter | solution.py:38
  84.2 10.2 all-to-all-start.2
  94.5 1.1 reshape.239
  97.6 142.3 %all-gather.10.cloned.1.call-done = bf16[16384,64]{1,0:T(8,128)(2,1)} async-done(((bf16[2048,64]{1,0:T(8,128)(2,1)}), bf16[16384,64]{1,0:T(8,128)(2,1)}) %all-gather.10.cloned.1.call-update) | async-done | bytes 2097168 | tf_op jit(solution)/shard_map/all_gather | solution.py:72
  239.9 3.9 copy.68
  243.8 13.3 %gather_fusion.1 = bf16[384,128,64]{1,2,0:T(8,128)(2,1)} fusion(bf16[128,128,64]{1,2,0:T(8,128)(2,1)S(1)} %copy.68, s32[1024]{0:T(1024)S(1)} %pad_clamp_fusion), kind=kCustom, calls=%fused_computation.1 | custom fusion | bytes 12584448 | tf_op jit(solution)/shard_map/gather | solution.py:15
  257.8 3.1 convolution_bitcast_fusion.5
  260.9 4.3 broadcast.110.clone.2
  265.2 9.0 scatter_fusion
  274.2 9.2 convert_reduce_fusion
  283.5 2.5 scatter_custom_fusion.5
  286.7 14.3 %fusion.38 = f32[384,128,64]{1,2,0:T(8,128)} fusion(bf16[384,128,64]{1,2,0:T(8,128)(2,1)} %gather_fusion.1, bf16[384,128,128]{2,1,0:T(8,128)(2,1)} %bitcast.9), kind=kOutput, calls=%fused_computation.120 | convolution fusion | flops 805306368 | bytes 31457280 | tf_op jit(solution)/shard_map/nab,nak->nbk/dot_general | solution.py:14
  301.0 4.3 broadcast.110.clone.3
  305.3 59.8 %scatter_fusion.3 = f32[256,128,64]{1,2,0:T(8,128)} fusion(f32[256,128,64]{1,2,0:T(8,128)} %broadcast.110.clone.3, s32[384]{0:T(512)S(1)} %get-tuple-element.8, f32[384,128,64]{1,2,0:T(8,128)} %fusion.38), kind=kCustom, calls=%fused_computation.9 | custom fusion | flops 3145728 | bytes 37750272 | tf_op jit(solution)/shard_map/scatter-add | solution.py:17
  365.1 8.6 copy_bitcast_fusion.2
  375.0 8.3 all-reduce.3.cloned.1.call-done
  384.0 84.0 %reduce-scatter.4.cloned.1.call-done = bf16[2048,64]{0,1:T(8,128)(2,1)} async-done(((bf16[32768,64]{0,1:T(8,128)(2,1)}), bf16[2048,64]{0,1:T(8,128)(2,1)}) %reduce-scatter.4.cloned.1.call-update) | async-done | bytes 262160 | tf_op jit(solution)/shard_map/reduce_scatter | solution.py:79
  468.0 2.3 fusion.5
  470.4 68.3 %all-gather.16.cloned.1.call-done = f32[8192,64]{1,0:T(8,128)} async-done(((f32[64,64]{1,0:T(8,128)}), f32[8192,64]{1,0:T(8,128)}) %all-gather.16.cloned.1.call-update) | async-done | bytes 2097168 | tf_op jit(solution)/shard_map/all_gather | solution.py:90
  538.8 2.5 reduce_sum.63
  541.5 5.8 cholesky.59
  548.7 4.9 custom-call.11
  554.8 16.3 %all_to_all.25 = bf16[128,2,512]{2,1,0:T(2,128)(2,1)S(1)} all-to-all(bf16[128,2,512]{2,1,0:T(2,128)(2,1)S(1)} %reshape.240), channel_id=1, replica_groups=mesh['row'=8,'col'=16] {'row','col'}, dimensions={0} | all-to-all | bytes 524288 | tf_op jit(solution)/shard_map/all_to_all | solution.py:65
  572.3 28.8 %all-gather.12.cloned.1.call-done = bf16[16384,64]{1,0:T(8,128)(2,1)} async-done(((bf16[2048,64]{1,0:T(8,128)(2,1)}), bf16[16384,64]{1,0:T(8,128)(2,1)}) %all-gather.12.cloned.1.call-update) | async-done | bytes 2097168 | tf_op jit(solution)/shard_map/all_gather | solution.py:72
  601.2 3.8 copy.78
  605.0 13.3 %gather_fusion.3 = bf16[384,128,64]{1,2,0:T(8,128)(2,1)} fusion(bf16[128,128,64]{1,2,0:T(8,128)(2,1)S(1)} %copy.78, s32[1024]{0:T(1024)S(1)} %pad_clamp_fusion), kind=kCustom, calls=%fused_computation.3 | custom fusion | bytes 12584448 | tf_op jit(solution)/shard_map/gather | solution.py:15
  619.1 14.4 %fusion.39 = f32[384,128,64]{1,2,0:T(8,128)} fusion(bf16[384,128,64]{1,2,0:T(8,128)(2,1)} %gather_fusion.3, bf16[384,128,128]{2,1,0:T(8,128)(2,1)} %bitcast.9), kind=kOutput, calls=%fused_computation.121 | convolution fusion | flops 805306368 | bytes 31457280 | tf_op jit(solution)/shard_map/nab,nak->nbk/dot_general | solution.py:14
  633.5 1.5 convolution_bitcast_fusion.4
  635.0 4.3 broadcast.110.clone.4
  639.3 59.8 %scatter_fusion.5 = f32[256,128,64]{1,2,0:T(8,128)} fusion(f32[256,128,64]{1,2,0:T(8,128)} %broadcast.110.clone.4, s32[384]{0:T(512)S(1)} %get-tuple-element.8, f32[384,128,64]{1,2,0:T(8,128)} %fusion.39), kind=kCustom, calls=%fused_computation.13 | custom fusion | flops 3145728 | bytes 37750272 | tf_op jit(solution)/shard_map/scatter-add | solution.py:17
  699.1 4.3 broadcast.110.clone.1
  703.4 9.2 scatter_fusion.4
  712.6 8.6 copy_bitcast_fusion.1
  721.2 75.8 %reduce-scatter.6.cloned.1.call-done = bf16[2048,64]{0,1:T(8,128)(2,1)} async-done(((bf16[32768,64]{0,1:T(8,128)(2,1)}), bf16[2048,64]{0,1:T(8,128)(2,1)}) %reduce-scatter.6.cloned.1.call-update) | async-done | bytes 262160 | tf_op jit(solution)/shard_map/reduce_scatter | solution.py:79
  797.1 2.3 fusion.6
  799.5 68.4 %all-gather.18.cloned.1.call-done = f32[8192,64]{1,0:T(8,128)} async-done(((f32[64,64]{1,0:T(8,128)}), f32[8192,64]{1,0:T(8,128)}) %all-gather.18.cloned.1.call-update) | async-done | bytes 2097168 | tf_op jit(solution)/shard_map/all_gather | solution.py:90
  867.8 2.5 reduce_sum.64
  870.5 5.8 cholesky.70
  877.7 4.9 custom-call.12
  883.9 16.3 %all_to_all.26 = bf16[128,2,512]{2,1,0:T(2,128)(2,1)S(1)} all-to-all(bf16[128,2,512]{2,1,0:T(2,128)(2,1)S(1)} %reshape.242), channel_id=1, replica_groups=mesh['row'=8,'col'=16] {'row','col'}, dimensions={0} | all-to-all | bytes 524288 | tf_op jit(solution)/shard_map/all_to_all | solution.py:65
  901.4 28.8 %all-gather.14.cloned.1.call-done = bf16[16384,64]{1,0:T(8,128)(2,1)} async-done(((bf16[2048,64]{1,0:T(8,128)(2,1)}), bf16[16384,64]{1,0:T(8,128)(2,1)}) %all-gather.14.cloned.1.call-update) | async-done | bytes 2097168 | tf_op jit(solution)/shard_map/all_gather | solution.py:72
  930.2 3.7 copy.85
  933.9 13.3 %gather_fusion.5 = bf16[384,128,64]{1,2,0:T(8,128)(2,1)} fusion(bf16[128,128,64]{1,2,0:T(8,128)(2,1)S(1)} %copy.85, s32[1024]{0:T(1024)S(1)} %pad_clamp_fusion), kind=kCustom, calls=%fused_computation.5 | custom fusion | bytes 12584448 | tf_op jit(solution)/shard_map/gather | solution.py:15
  948.0 14.4 %fusion.40 = f32[384,128,64]{1,2,0:T(8,128)} fusion(bf16[384,128,64]{1,2,0:T(8,128)(2,1)} %gather_fusion.5, bf16[384,128,128]{2,1,0:T(8,128)(2,1)} %bitcast.9), kind=kOutput, calls=%fused_computation.122 | convolution fusion | flops 805306368 | bytes 31457280 | tf_op jit(solution)/shard_map/nab,nak->nbk/dot_general | solution.py:14
  962.4 1.5 convolution_bitcast_fusion.3
  963.9 4.3 broadcast.110.clone.5
  968.2 58.9 %scatter_fusion.7 = f32[256,128,64]{1,2,0:T(8,128)} fusion(f32[256,128,64]{1,2,0:T(8,128)} %broadcast.110.clone.5, s32[384]{0:T(512)S(1)} %get-tuple-element.8, f32[384,128,64]{1,2,0:T(8,128)} %fusion.40), kind=kCustom, calls=%fused_computation.15 | custom fusion | flops 3145728 | bytes 37750272 | tf_op jit(solution)/shard_map/scatter-add | solution.py:17
  1027.1 4.3 broadcast.110.clone
  1031.4 9.2 scatter_fusion.6
  1040.6 8.5 copy_bitcast_fusion
  1049.2 75.4 %reduce-scatter.8.cloned.1.call-done = bf16[2048,64]{0,1:T(8,128)(2,1)} async-done(((bf16[32768,64]{0,1:T(8,128)(2,1)}), bf16[2048,64]{0,1:T(8,128)(2,1)}) %reduce-scatter.8.cloned.1.call-update) | async-done | bytes 262160 | tf_op jit(solution)/shard_map/reduce_scatter | solution.py:79
  1124.6 2.3 fusion.7
  1127.0 68.4 %all-gather.20.cloned.1.call-done = f32[8192,64]{1,0:T(8,128)} async-done(((f32[64,64]{1,0:T(8,128)}), f32[8192,64]{1,0:T(8,128)}) %all-gather.20.cloned.1.call-update) | async-done | bytes 2097168 | tf_op jit(solution)/shard_map/all_gather | solution.py:90
  1195.4 2.5 reduce_sum.65
  1198.1 5.8 cholesky.81
  1205.3 4.9 custom-call.13
  1210.2 1.4 convolution_bitcast_fusion
  (92 shorter events, 17.9 us)
Async XLA Ops:
  20.0 21.6 %all-to-all-start.1 = ((s32[128,3,2]{1,2,0:T(2,128)}), s32[128,3,2]{1,2,0:T(2,128)S(1)}, u32[]{:S(2)}, u32[]{:S(2)}) async-start(s32[128,3,2]{1,2,0:T(2,128)} %copy.70), calls=%async_computation.1 | async-start | bytes 262144 | tf_op jit(solution)/shard_map/all_to_all | solution.py:44
  41.6 42.6 %all-to-all-start = ((bf16[128,2,512]{2,1,0:T(2,128)(2,1)}), bf16[128,2,512]{2,1,0:T(2,128)(2,1)S(1)}, u32[]{:S(2)}, u32[]{:S(2)}) async-start(bf16[128,2,512]{2,1,0:T(2,128)(2,1)} %reshape.238), calls=%async_computation | async-start | bytes 524288 | tf_op jit(solution)/shard_map/all_to_all | solution.py:65
  84.2 11.5 copy-start.6
  84.2 11.6 copy-start
  84.2 13.1 %copy-start.7 = (s32[64]{0:T(128)S(1)}, s32[64]{0:T(128)}, u32[]{:S(2)}) copy-start(s32[64]{0:T(128)} %param.13) | copy-start | bytes 772
  84.2 190.0 %all-to-all-start.2 = ((bf16[128,3,128,128]{3,2,1,0:T(8,128)(2,1)}), bf16[128,3,128,128]{3,2,1,0:T(8,128)(2,1)}, u32[]{:S(2)}, u32[]{:S(2)}) async-start(bf16[128,3,128,128]{3,2,1,0:T(8,128)(2,1)} %scatter_fusion.2), calls=%async_computation.2 | async-start | bytes 25165824 | tf_op jit(solution)/shard_map/all_to_all | solution.py:43
  94.5 145.4 %all-gather.10.cloned.1.call-start = ((), (), s32[]{:S(2)}) async-start(), calls=%async_computation.8 | async-start | bytes 4718592 | tf_op jit(solution)/shard_map/all_gather | solution.py:72
  95.7 287.6 %all-reduce.3.cloned.1.call-start = ((), (), s32[]{:S(2)}) async-start(), calls=%async_computation.17 | async-start | bytes 131072
  286.7 181.4 %reduce-scatter.4.cloned.1.call-start = ((), (), s32[]{:S(2)}) async-start(), calls=%async_computation.9 | async-start | bytes 4456448 | tf_op jit(solution)/shard_map/reduce_scatter | solution.py:79
  365.1 8.7 copy-start.8
  373.7 165.1 %all-gather.16.cloned.1.call-start = ((), (), s32[]{:S(2)}) async-start(), calls=%async_computation.14 | async-start | bytes 4227072 | tf_op jit(solution)/shard_map/all_gather | solution.py:90
  468.0 85.6 %copy-start.3 = (bf16[2048,64]{0,1:T(8,128)(2,1)S(1)}, bf16[2048,64]{0,1:T(8,128)(2,1)}, u32[]{:S(2)}) copy-start(bf16[2048,64]{0,1:T(8,128)(2,1)} %reduce-scatter.4.cloned.1.call-done) | copy-start | bytes 786436
  470.4 130.8 %all-gather.12.cloned.1.call-start = ((), (), s32[]{:S(2)}) async-start(), calls=%async_computation.10 | async-start | bytes 4718592 | tf_op jit(solution)/shard_map/all_gather | solution.py:72
  572.3 224.8 %reduce-scatter.6.cloned.1.call-start = ((), (), s32[]{:S(2)}) async-start(), calls=%async_computation.11 | async-start | bytes 4456448 | tf_op jit(solution)/shard_map/reduce_scatter | solution.py:79
  619.0 14.4 %copy-start.1 = (bf16[64,128,128]{2,1,0:T(8,128)(2,1)S(1)}, bf16[64,128,128]{2,1,0:T(8,128)(2,1)}, u32[]{:S(2)}) copy-start(bf16[64,128,128]{2,1,0:T(8,128)(2,1)} %param.11) | copy-start | bytes 6291460
  721.2 146.6 %all-gather.18.cloned.1.call-start = ((), (), s32[]{:S(2)}) async-start(), calls=%async_computation.15 | async-start | bytes 4227072 | tf_op jit(solution)/shard_map/all_gather | solution.py:90
  797.1 85.6 %copy-start.4 = (bf16[2048,64]{0,1:T(8,128)(2,1)S(1)}, bf16[2048,64]{0,1:T(8,128)(2,1)}, u32[]{:S(2)}) copy-start(bf16[2048,64]{0,1:T(8,128)(2,1)} %reduce-scatter.6.cloned.1.call-done) | copy-start | bytes 786436
  799.4 130.8 %all-gather.14.cloned.1.call-start = ((), (), s32[]{:S(2)}) async-start(), calls=%async_computation.12 | async-start | bytes 4718592 | tf_op jit(solution)/shard_map/all_gather | solution.py:72
  901.3 223.3 %reduce-scatter.8.cloned.1.call-start = ((), (), s32[]{:S(2)}) async-start(), calls=%async_computation.13 | async-start | bytes 4456448 | tf_op jit(solution)/shard_map/reduce_scatter | solution.py:79
  947.9 14.4 %copy-start.2 = (bf16[64,128,128]{2,1,0:T(8,128)(2,1)S(1)}, bf16[64,128,128]{2,1,0:T(8,128)(2,1)}, u32[]{:S(2)}) copy-start(bf16[64,128,128]{2,1,0:T(8,128)(2,1)} %param.11) | copy-start | bytes 6291460
  1049.2 146.2 %all-gather.20.cloned.1.call-start = ((), (), s32[]{:S(2)}) async-start(), calls=%async_computation.16 | async-start | bytes 4227072 | tf_op jit(solution)/shard_map/all_gather | solution.py:90
  1124.6 85.6 %copy-start.5 = (bf16[2048,64]{0,1:T(8,128)(2,1)S(1)}, bf16[2048,64]{0,1:T(8,128)(2,1)}, u32[]{:S(2)}) copy-start(bf16[2048,64]{0,1:T(8,128)(2,1)} %reduce-scatter.8.cloned.1.call-done) | copy-start | bytes 786436
Sparse Core Ops, SparseCore 0:
  97.1 142.6 all-gather.9
  470.5 68.2 all-gather.15
  572.4 28.7 all-gather.11
  799.5 68.2 all-gather.17
  901.5 28.7 all-gather.13
  1127.1 68.2 all-gather.19
Sparse Core Ops, SparseCore 1:
  286.7 96.5 all-reduce.2
  386.9 81.1 reduce-scatter.3
  721.3 75.7 reduce-scatter.5
  1049.3 75.3 reduce-scatter.7
